TPU v7x, 32 devices: a whole 2x2x4 slice. The times are simulated.
32 devices in a mesh: slab: 4 (over y, core), row: 2 (over x), col: 4 (over z).
Axes of the slice: x: 2, y: 2, z: 4, core: 2. Of those that a mesh axis runs over, the one named last changes fastest.
Arguments:
- reflection: bfloat16 [4, 4096, 4096], P('slab', 'row', 'col'), may hold values from -0.0625 to 0.0625
- transmission: bfloat16 [4, 4096, 4096], P('slab', 'row', 'col'), may hold values from -0.09375 to 0.09375
- shots: bfloat16 [4, 4096, 1024], P('slab', 'row', 'col'), may hold values from -6 to 6
Outputs:
- merged: bfloat16 [4, 4096, 1024], P('slab', 'row', 'col')
All inputs are finite; a program needn't handle non-finite values.
Results may differ from a plain program's by a relative error of at most 0.008.
Values may be sent and summed in bfloat16 or wider, within the bound.
A program may use at most 128 MiB of HBM per device.

v0:
```python
import jax
import jax.numpy as jnp
from jax import lax
from jax.experimental import pallas as pl
from jax.experimental.pallas import tpu as pltpu
from jax.sharding import PartitionSpec as P

GROUPS = 2


def partner(block, axis, bit):
    count = lax.axis_size(axis)
    route = []
    for low in range(count):
        high = low | 1 << bit
        if high != low and high < count:
            route += [(low, high), (high, low)]
    return lax.ppermute(block, axis, route)


def shift(block, axis, by):
    count = lax.axis_size(axis)
    by %= count
    if by == 0:
        return block
    return lax.ppermute(block, axis, [(i, (i + by) % count) for i in range(count)])


def pick(options, place):
    chosen = options[0]
    for at in range(1, len(options)):
        chosen = jnp.where(place == at, options[at], chosen)
    return chosen


def in_order(relative, me):
    count = len(relative)
    return [pick([relative[(j - at) % count] for at in range(count)], me) for j in range(count)]


def dot(a, b):
    return jnp.dot(a, b, preferred_element_type=jnp.float32)


def on_device(reflection, transmission, shots):
    own_refl = reflection[0]
    own_trans = transmission[0]
    shot_tile = shots[0]
    rows, cols = lax.axis_size("row"), lax.axis_size("col")
    x = lax.axis_index("row")
    bf16 = jnp.bfloat16
    far_refl, far_trans = partner((own_refl, own_trans), "slab", 0)

    width = shot_tile.shape[1] // rows
    kept = []
    for k in range(rows):
        piece = lax.dynamic_slice_in_dim(shot_tile, ((x + k) % rows) * width, width, axis=1)
        kept.append(shift(piece, "row", k))
    face = jnp.concatenate(in_order([kept[-k % rows] for k in range(rows)], x), axis=0)
    depth = face.shape[0] // cols
    face = lax.all_to_all(face.reshape(cols, depth, width), "col", 0, 0)

    groups = GROUPS if cols % GROUPS == 0 else 1
    per = cols // groups
    state = []
    for g in range(groups):
        mine = jnp.concatenate([face[g * per + i] for i in range(per)], axis=1)
        state.append(mine)

    def product(operator, mine):
        pieces = [shift(mine, "row", k) for k in range(rows)]
        sent = [
            shift(dot(operator, pieces[k]).astype(bf16), "row", -k) for k in range(rows)
        ]
        whole = jnp.concatenate(in_order(sent, x), axis=0)
        return lax.psum_scatter(whole, "col", scatter_dimension=0, tiled=True)

    first = [product(own_trans, mine) for mine in state]
    middle = [product(far_refl, mine) for mine in first]
    bounce = [product(own_refl, mine) for mine in middle]
    summed = [
        (a.astype(jnp.float32) + b.astype(jnp.float32)).astype(bf16)
        for a, b in zip(first, bounce)
    ]
    panels = []
    for mine in summed:
        pieces = [shift(mine, "row", k) for k in range(rows)]
        ordered = in_order([pieces[-k % rows] for k in range(rows)], x)
        for i in range(per):
            panels.append(
                jnp.concatenate([o[:, i * width : (i + 1) * width] for o in ordered], axis=1)
            )
    merged = jnp.stack([dot(far_trans, p).astype(bf16) for p in panels])
    merged = lax.psum_scatter(merged, "col", scatter_dimension=0, tiled=True)
    return merged


F32, BF16 = jnp.float32, jnp.bfloat16
ORDER = (0, 3, 1, 2)
LAST = 3
MESH = pl.DeviceIdType.MESH


def chain_kernel(
    refl, trans, shots, out, ops, faces, kept, stage, parts, far, near, far_last, near_last,
    load_sem, core_send, core_recv, init_send, init_recv, face_send, face_recv,
    part_send, part_recv, col_send, far_recv, near_recv,
    last_send, last_far_recv, last_near_recv,
):
    s, x, z = lax.axis_index("slab"), lax.axis_index("row"), lax.axis_index("col")
    other_slab = s + 1 - 2 * (s % 2)
    other_x = 1 - x
    height = trans.shape[0]
    depth = faces.shape[2]
    lanes = faces.shape[3]
    high = z // 2
    end = (z == 0) | (z == 3)
    inner = (z == 1) | (z == 2)

    def blk(k):
        return k + high * (3 - 2 * k)

    def remote(src, dst, send, recv, **where):
        return pltpu.make_async_remote_copy(
            src_ref=src, dst_ref=dst, send_sem=send, recv_sem=recv,
            device_id=where, device_id_type=MESH,
        )

    barrier = pltpu.get_barrier_semaphore()
    pl.semaphore_signal(barrier, inc=1, device_id={"slab": other_slab}, device_id_type=MESH)
    for step in range(1, 8):
        place = (x * 4 + z + step) % 8
        pl.semaphore_signal(
            barrier, inc=1, device_id={"row": place // 4, "col": place % 4}, device_id_type=MESH
        )
    pl.semaphore_wait(barrier, 8)

    loads = [
        pltpu.make_async_copy(trans, ops.at[0], load_sem.at[0]),
        pltpu.make_async_copy(refl, ops.at[2], load_sem.at[1]),
    ]
    for copy in loads:
        copy.start()

    def spread(b, c):
        return shots.at[pl.ds(b * depth, depth), pl.ds(c * lanes, lanes)]

    spots = [(b, c) for b in range(2) for c in range(2)]

    def hand_out(mine):
        for at, (b, c) in enumerate(spots):
            here = (z == 2 * x + b) & (x == c)
            target = faces.at[z, c]

            @pl.when(mine & here)
            def _():
                pltpu.make_async_copy(spread(b, c), target, init_recv.at[z]).start()

            @pl.when(mine & jnp.logical_not(here))
            def _():
                remote(
                    spread(b, c), target, init_send.at[at], init_recv.at[z],
                    row=jnp.int32(c), col=2 * x + b,
                ).start()

    hand_out(end)
    hand_out(inner)

    swaps = [
        remote(refl, ops.at[1], core_send.at[0], core_recv.at[0], slab=other_slab),
        remote(trans, ops.at[3], core_send.at[1], core_recv.at[1], slab=other_slab),
    ]
    for copy in swaps:
        copy.start()

    def face_copy(p, g):
        return remote(
            faces.at[g, x], faces.at[g, x], face_send.at[p, g], face_recv.at[p, g], row=other_x
        )

    def face_wait(p, g):
        return remote(
            faces.at[g, other_x], faces.at[g, other_x], face_send.at[p, g], face_recv.at[p, g],
            row=other_x,
        ).wait_recv()

    def half(p, g, which):
        return parts.at[p % 2, g, pl.ds(2 * which, 2)]

    def part_copy(p, g, which):
        return remote(
            stage.at[g], half(p, g, which), part_send.at[p, g], part_recv.at[p, g], row=other_x
        )

    def gather(g):
        pltpu.make_async_copy(faces.at[g, x], faces.at[g, x], init_recv.at[g]).wait()
        face_copy(0, g).start()

    tile = min(depth, 512)
    steps = height // tile
    per = depth // tile

    def multiply(p, g):
        if p == 0 and g == ORDER[0]:
            loads[0].wait()
        if p == 1 and g == ORDER[0]:
            swaps[0].wait_recv()
        if p == 2 and g == ORDER[0]:
            loads[1].wait()
        if p == LAST and g == ORDER[0]:
            swaps[1].wait_recv()
        face_wait(p, g)
        if p < LAST:
            if p > 0:
                part_copy(p - 1, g, x).wait_send()
            both = jnp.concatenate([faces[g, other_x], faces[g, x]], axis=1)
        else:
            both = jnp.concatenate([faces[g, 0], faces[g, 1]], axis=1)

        def body(i, carry):
            rows = pl.multiple_of(i * tile, tile)
            block = i // per
            inside = pl.multiple_of((i % per) * tile, tile)
            value = jnp.dot(
                ops[p, pl.ds(rows, tile), :], both, preferred_element_type=F32
            ).astype(BF16)
            if p < LAST:
                stage[g, block, pl.ds(inside, tile), :] = value[:, :lanes]
                parts[p % 2, g, 2 * x + block, pl.ds(inside, tile), :] = value[:, lanes:]
            else:
                parts[p % 2, g, block, pl.ds(inside, tile), :] = value[:, :lanes]
                parts[p % 2, g, 2 + block, pl.ds(inside, tile), :] = value[:, lanes:]
            return carry

        lax.fori_loop(0, steps, body, 0)
        if p < LAST:
            part_copy(p, g, x).start()

    def block_copy(p, g, k, slot, bank, sems, to, at):
        return remote(
            parts.at[p % 2, g, blk(k)], bank.at[p % 2, g, at],
            col_send.at[p, g, slot], sems.at[p, g, at], col=blk(to),
        )

    def end_copies(p, g):
        return [
            block_copy(p, g, 3, 0, far, far_recv, 1, 0),
            block_copy(p, g, 2, 1, far, far_recv, 1, 1),
            block_copy(p, g, 1, 2, near, near_recv, 1, 0),
        ]

    def inner_copies(p, g):
        return [
            block_copy(p, g, 0, 0, near, near_recv, 0, 0),
            block_copy(p, g, 3, 1, near, near_recv, 3, 1),
            block_copy(p, g, 2, 2, near, near_recv, 2, 1),
        ]

    def last_far(g, b, to):
        return remote(
            parts.at[1, g, b], far_last.at[g, b], last_send.at[g, b, 0], last_far_recv.at[g, b],
            col=to,
        )

    def last_near(g, b, at, to):
        return remote(
            parts.at[1, g, b], near_last.at[at, b], last_send.at[g, b, 1 + at],
            last_near_recv.at[at, b], col=to,
        )

    def is_blk(g, *ks):
        hit = blk(ks[0]) == g
        for k in ks[1:]:
            hit = hit | (blk(k) == g)
        return hit

    def settle(p, g):
        @pl.when(end)
        def _():
            for copy in end_copies(p, g):
                copy.wait_send()

        @pl.when(inner)
        def _():
            for copy in inner_copies(p, g):
                copy.wait_send()

    def begin(p, g):
        if p == LAST:
            @pl.when(end & is_blk(g, 2, 3))
            def _():
                for b in range(4):
                    last_far(g, b, blk(1)).start()

            @pl.when(end & is_blk(g, 1))
            def _():
                for b in range(4):
                    last_near(g, b, 0, blk(1)).start()

            @pl.when(inner & is_blk(g, 0))
            def _():
                for b in range(4):
                    last_near(g, b, 0, blk(0)).start()

            return
        if p > 0:
            settle(p - 1, g)
        remote(
            stage.at[g], half(p, g, other_x), part_send.at[p, g], part_recv.at[p, g], row=other_x
        ).wait_recv()

        @pl.when(end)
        def _():
            for copy in end_copies(p, g):
                copy.start()

        @pl.when(inner)
        def _():
            inner_copies(p, g)[0].start()

    def merge(p, g):
        if p == LAST:
            @pl.when(inner & is_blk(g, 2, 3))
            def _():
                for b in range(4):
                    last_far(g, b, blk(1)).wait_recv()
                    parts[1, g, b] = (
                        parts[1, g, b].astype(F32) + far_last[g, b].astype(F32)
                    ).astype(BF16)
                    last_near(g, b, 1, jnp.int32(g)).start()

            return

        @pl.when(inner)
        def _():
            arrive = end_copies(p, g)
            leave = inner_copies(p, g)
            for at, k in ((0, 3), (1, 2)):
                arrive[at].wait_recv()
                parts[p % 2, g, blk(k)] = (
                    parts[p % 2, g, blk(k)].astype(F32) + far[p % 2, g, at].astype(F32)
                ).astype(BF16)
                leave[1 + at].start()

    def finish(p, g):
        if p == LAST:
            return
        for at in range(2):
            block_copy(p, g, 0, 0, near, near_recv, 0, at).wait_recv()
        total = (
            parts[p % 2, g, z].astype(F32)
            + near[p % 2, g, 0].astype(F32)
            + near[p % 2, g, 1].astype(F32)
        )
        face_copy(p, g).wait_send()
        if p == 0:
            kept[g] = total.astype(BF16)
        if p == 2:
            total = total + kept[g].astype(F32)
        faces[g, x] = total.astype(BF16)
        face_copy(p + 1, g).start()

    order = [(p, g) for p in range(LAST + 1) for g in ORDER]
    for g in ORDER[:2]:
        gather(g)
    multiply(*order[0])
    for g in ORDER[2:]:
        gather(g)
    count = len(order)
    for t in range(count + 2):
        if t < count:
            begin(*order[t])
        if 0 <= t - 1 < count:
            merge(*order[t - 1])
        if t + 1 < count:
            multiply(*order[t + 1])
        if 0 <= t - 2 < count:
            finish(*order[t - 2])

    for g in range(4):
        @pl.when(z == g)
        def _():
            for b in range(4):
                for at in range(2):
                    last_near(g, b, at, z).wait_recv()
                c, h = b // 2, b % 2
                out[pl.ds(h * depth, depth), pl.ds(c * lanes, lanes)] = (
                    parts[1, g, b].astype(F32)
                    + near_last[0, b].astype(F32)
                    + near_last[1, b].astype(F32)
                ).astype(BF16)

    for g in range(4):
        settle(LAST - 1, g)
        face_copy(LAST, g).wait_send()
        part_copy(LAST - 1, g, x).wait_send()

        @pl.when(end & is_blk(g, 2, 3))
        def _():
            for b in range(4):
                last_far(g, b, blk(1)).wait_send()

        @pl.when(end & is_blk(g, 1))
        def _():
            for b in range(4):
                last_near(g, b, 0, blk(1)).wait_send()

        @pl.when(inner & is_blk(g, 0))
        def _():
            for b in range(4):
                last_near(g, b, 0, blk(0)).wait_send()

        @pl.when(inner & is_blk(g, 2, 3))
        def _():
            for b in range(4):
                last_near(g, b, 1, jnp.int32(g)).wait_send()

    for copy in swaps:
        copy.wait_send()
    for at, (b, c) in enumerate(spots):
        here = (z == 2 * x + b) & (x == c)

        @pl.when(jnp.logical_not(here))
        def _():
            remote(
                spread(b, c), faces.at[z, c], init_send.at[at], init_recv.at[z],
                row=jnp.int32(c), col=2 * x + b,
            ).wait_send()


def chain(reflection, transmission, shots):
    refl, trans, tile = reflection[0], transmission[0], shots[0]
    height, inner = trans.shape
    lanes = tile.shape[1] // 2
    hbm = pl.BlockSpec(memory_space=pl.ANY)
    dma = pltpu.SemaphoreType.DMA
    block = (inner, lanes)
    out = pl.pallas_call(
        chain_kernel,
        out_shape=jax.ShapeDtypeStruct(tile.shape, BF16),
        in_specs=[hbm] * 3,
        out_specs=pl.BlockSpec(memory_space=pltpu.VMEM),
        scratch_shapes=[
            pltpu.VMEM((4, height, inner), BF16),
            pltpu.VMEM((4, 2) + block, BF16),
            pltpu.VMEM((4,) + block, BF16),
            pltpu.VMEM((4, 2) + block, BF16),
            pltpu.VMEM((2, 4, 4) + block, BF16),
            pltpu.VMEM((2, 4, 2) + block, BF16),
            pltpu.VMEM((2, 4, 2) + block, BF16),
            pltpu.VMEM((4, 4) + block, BF16),
            pltpu.VMEM((2, 4) + block, BF16),
            dma((2,)), dma((2,)), dma((2,)), dma((4,)), dma((4,)),
            dma((4, 4)), dma((4, 4)), dma((3, 4)), dma((3, 4)),
            dma((3, 4, 3)), dma((3, 4, 2)), dma((3, 4, 2)),
            dma((4, 4, 3)), dma((4, 4)), dma((2, 4)),
        ],
        compiler_params=pltpu.CompilerParams(
            collective_id=0, has_side_effects=True, vmem_limit_bytes=60 << 20
        ),
    )(refl, trans, tile)
    return out[None]


def on_slice(reflection, transmission, shots):
    height, inner = transmission.shape[1:]
    fits = (
        lax.axis_size("row") == 2
        and lax.axis_size("col") == 4
        and height == 2 * inner
        and inner % 512 == 0
        and shots.shape[2] % 256 == 0
        and 11 * height * inner < 24 << 20
    )
    if fits:
        return chain(reflection, transmission, shots)
    return on_device(reflection, transmission, shots)


def solution(mesh):
    placed = (P("slab", "row", "col"), P("slab", "row", "col"), P("slab", "row", "col"))
    return jax.shard_map(
        on_slice, mesh=mesh, in_specs=placed, out_specs=P("slab", "row", "col"), check_vma=False
    )
```

profile of v0, /device:TPU:18, one launch (start us, length us, event | category | flops | bytes accessed | tf_op | source)
XLA Modules:
  0.0 338.8 jit_solution(16712371125749909371)
XLA Ops:
  0.0 336.5 %shard_map.37 = bf16[2048,256]{1,0:T(8,128)(2,1)} custom-call(bf16[2048,1024]{1,0:T(8,128)(2,1)} %bitcast.5, bf16[2048,1024]{1,0:T(8,128)(2,1)} %bitcast.6, bf16[2048,256]{1,0:T(8,128)(2,1)} %bitcast.7), custom_call_target="tpu_custom_call" | custom-call | tf_op jit(solution)/shard_map/pallas_call | solution.py:438
  336.5 2.3 copy.5
where the time goes:
time: 342 us; the launch traced here: 339 us
  Pallas kernels  336 us (98%)
    pallas_call x1, Pallas kernels, chain(): pl.pallas_call(chain_kernel, out_shape=jax.ShapeDtypeStruct(tile.shape, B...  336 us

commit v1 on v0

--- a/solution.py
+++ b/solution.py
@@ -102,8 +102,8 @@
 
 
 def chain_kernel(
-    refl, trans, shots, out, ops, faces, kept, stage, parts, far, near, far_last, near_last,
-    load_sem, core_send, core_recv, init_send, init_recv, face_send, face_recv,
+    refl, trans, shots, out, ops, inbox, faces, kept, stage, parts, far, near, far_last, near_last,
+    load_sem, core_send, core_recv, cross_send, cross_recv, init_send, init_recv, face_send, face_recv,
     part_send, part_recv, col_send, far_recv, near_recv,
     last_send, last_far_recv, last_near_recv,
 ):
@@ -142,29 +142,35 @@
     for copy in loads:
         copy.start()
 
-    def spread(b, c):
-        return shots.at[pl.ds(b * depth, depth), pl.ds(c * lanes, lanes)]
-
-    spots = [(b, c) for b in range(2) for c in range(2)]
-
-    def hand_out(mine):
-        for at, (b, c) in enumerate(spots):
-            here = (z == 2 * x + b) & (x == c)
-            target = faces.at[z, c]
-
-            @pl.when(mine & here)
-            def _():
-                pltpu.make_async_copy(spread(b, c), target, init_recv.at[z]).start()
-
-            @pl.when(mine & jnp.logical_not(here))
-            def _():
-                remote(
-                    spread(b, c), target, init_send.at[at], init_recv.at[z],
-                    row=jnp.int32(c), col=2 * x + b,
-                ).start()
-
-    hand_out(end)
-    hand_out(inner)
+    def shot_block(b, c):
+        return shots.at[pl.ds(b * depth, depth), pl.ds(pl.multiple_of(c * lanes, lanes), lanes)]
+
+    def cross(b):
+        return remote(
+            shot_block(b, other_x), inbox.at[b], cross_send.at[b], cross_recv.at[b], row=other_x
+        )
+
+    def hand_on(source, b, at, to, act):
+        @pl.when(to == z)
+        def _():
+            if act == "start":
+                pltpu.make_async_copy(source, faces.at[z, x], init_recv.at[z]).start()
+
+        @pl.when(to != z)
+        def _():
+            copy = remote(source, faces.at[z, x], init_send.at[at], init_recv.at[z], col=to)
+            copy.start() if act == "start" else copy.wait_send()
+
+    def own_block(b, act):
+        hand_on(shot_block(b, x), b, b, 2 * x + b, act)
+
+    def crossed_block(b, act):
+        hand_on(inbox.at[b], b, 2 + b, 2 * other_x + b, act)
+
+    for b in range(2):
+        cross(b).start()
+    for b in range(2):
+        own_block(b, "start")
 
     swaps = [
         remote(refl, ops.at[1], core_send.at[0], core_recv.at[0], slab=other_slab),
@@ -172,6 +178,9 @@
     ]
     for copy in swaps:
         copy.start()
+    for b in range(2):
+        cross(b).wait_recv()
+        crossed_block(b, "start")
 
     def face_copy(p, g):
         return remote(
@@ -417,15 +426,10 @@
 
     for copy in swaps:
         copy.wait_send()
-    for at, (b, c) in enumerate(spots):
-        here = (z == 2 * x + b) & (x == c)
-
-        @pl.when(jnp.logical_not(here))
-        def _():
-            remote(
-                spread(b, c), faces.at[z, c], init_send.at[at], init_recv.at[z],
-                row=jnp.int32(c), col=2 * x + b,
-            ).wait_send()
+    for b in range(2):
+        cross(b).wait_send()
+        own_block(b, "wait")
+        crossed_block(b, "wait")
 
 
 def chain(reflection, transmission, shots):
@@ -442,6 +446,7 @@
         out_specs=pl.BlockSpec(memory_space=pltpu.VMEM),
         scratch_shapes=[
             pltpu.VMEM((4, height, inner), BF16),
+            pltpu.VMEM((2,) + block, BF16),
             pltpu.VMEM((4, 2) + block, BF16),
             pltpu.VMEM((4,) + block, BF16),
             pltpu.VMEM((4, 2) + block, BF16),
@@ -450,7 +455,7 @@
             pltpu.VMEM((2, 4, 2) + block, BF16),
             pltpu.VMEM((4, 4) + block, BF16),
             pltpu.VMEM((2, 4) + block, BF16),
-            dma((2,)), dma((2,)), dma((2,)), dma((4,)), dma((4,)),
+            dma((2,)), dma((2,)), dma((2,)), dma((2,)), dma((2,)), dma((4,)), dma((4,)),
             dma((4, 4)), dma((4, 4)), dma((3, 4)), dma((3, 4)),
             dma((3, 4, 3)), dma((3, 4, 2)), dma((3, 4, 2)),
             dma((4, 4, 3)), dma((4, 4)), dma((2, 4)),

time: 342 us -> 329 us (0.962)
  Pallas kernels: 336 us -> 325 us
    pallas_call x1, Pallas kernels: 336 us -> 325 us  [chain(): pl.pallas_call(chain_kernel, out_shape=jax.ShapeDtypeStruct(tile.shape, B...]
where the time goes in v1:
time: 329 us; the launch traced here: 327 us
  Pallas kernels  325 us (99%)
    pallas_call x1, Pallas kernels, chain(): pl.pallas_call(chain_kernel, out_shape=jax.ShapeDtypeStruct(tile.shape, B...  325 us

profile of v1, /device:TPU:18, one launch (start us, length us, event | category | flops | bytes accessed | tf_op | source)
XLA Modules:
  0.0 327.5 jit_solution(12794575367649854394)
XLA Ops:
  0.0 325.2 %shard_map.37 = bf16[2048,256]{1,0:T(8,128)(2,1)} custom-call(bf16[2048,1024]{1,0:T(8,128)(2,1)} %bitcast.5, bf16[2048,1024]{1,0:T(8,128)(2,1)} %bitcast.6, bf16[2048,256]{1,0:T(8,128)(2,1)} %bitcast.7), custom_call_target="tpu_custom_call" | custom-call | tf_op jit(solution)/shard_map/pallas_call | solution.py:442
  325.2 2.3 copy.5

commit v2 on v1

--- a/solution.py
+++ b/solution.py
@@ -193,20 +193,21 @@
             row=other_x,
         ).wait_recv()
 
-    def half(p, g, which):
-        return parts.at[p % 2, g, pl.ds(2 * which, 2)]
-
-    def part_copy(p, g, which):
-        return remote(
-            stage.at[g], half(p, g, which), part_send.at[p, g], part_recv.at[p, g], row=other_x
-        )
+    def part_copy(p, g, j, which):
+        off = turn(j)
+        return remote(
+            stage.at[g, off], parts.at[p % 2, g, 2 * which + off],
+            part_send.at[p, g, j], part_recv.at[p, g, j], row=other_x,
+        )
+
+    def turn(j):
+        return 1 - high if j == 0 else high
 
     def gather(g):
         pltpu.make_async_copy(faces.at[g, x], faces.at[g, x], init_recv.at[g]).wait()
         face_copy(0, g).start()
 
     tile = min(depth, 512)
-    steps = height // tile
     per = depth // tile
 
     def multiply(p, g):
@@ -221,15 +222,16 @@
         face_wait(p, g)
         if p < LAST:
             if p > 0:
-                part_copy(p - 1, g, x).wait_send()
+                for j in range(2):
+                    part_copy(p - 1, g, j, x).wait_send()
+                settle(p - 1, g)
             both = jnp.concatenate([faces[g, other_x], faces[g, x]], axis=1)
         else:
             both = jnp.concatenate([faces[g, 0], faces[g, 1]], axis=1)
 
-        def body(i, carry):
-            rows = pl.multiple_of(i * tile, tile)
-            block = i // per
-            inside = pl.multiple_of((i % per) * tile, tile)
+        def body(i, block):
+            inside = pl.multiple_of(i * tile, tile)
+            rows = pl.multiple_of(block * depth + inside, tile)
             value = jnp.dot(
                 ops[p, pl.ds(rows, tile), :], both, preferred_element_type=F32
             ).astype(BF16)
@@ -239,11 +241,23 @@
             else:
                 parts[p % 2, g, block, pl.ds(inside, tile), :] = value[:, :lanes]
                 parts[p % 2, g, 2 + block, pl.ds(inside, tile), :] = value[:, lanes:]
-            return carry
-
-        lax.fori_loop(0, steps, body, 0)
-        if p < LAST:
-            part_copy(p, g, x).start()
+            return block
+
+        for j in range(2):
+            lax.fori_loop(0, per, body, turn(j))
+            if p < LAST:
+                part_copy(p, g, j, x).start()
+                send_block(p, g, 2 * x + turn(j))
+
+    def send_block(p, g, block):
+        for copy, k in zip(end_copies(p, g), (3, 2, 1)):
+            @pl.when(end & (block == blk(k)))
+            def _():
+                copy.start()
+
+        @pl.when(inner & (block == blk(0)))
+        def _():
+            inner_copies(p, g)[0].start()
 
     def block_copy(p, g, k, slot, bank, sems, to, at):
         return remote(
@@ -312,20 +326,9 @@
                     last_near(g, b, 0, blk(0)).start()
 
             return
-        if p > 0:
-            settle(p - 1, g)
-        remote(
-            stage.at[g], half(p, g, other_x), part_send.at[p, g], part_recv.at[p, g], row=other_x
-        ).wait_recv()
-
-        @pl.when(end)
-        def _():
-            for copy in end_copies(p, g):
-                copy.start()
-
-        @pl.when(inner)
-        def _():
-            inner_copies(p, g)[0].start()
+        for j in range(2):
+            part_copy(p, g, j, other_x).wait_recv()
+            send_block(p, g, 2 * other_x + turn(j))
 
     def merge(p, g):
         if p == LAST:
@@ -402,7 +405,8 @@
     for g in range(4):
         settle(LAST - 1, g)
         face_copy(LAST, g).wait_send()
-        part_copy(LAST - 1, g, x).wait_send()
+        for j in range(2):
+            part_copy(LAST - 1, g, j, x).wait_send()
 
         @pl.when(end & is_blk(g, 2, 3))
         def _():
@@ -456,7 +460,7 @@
             pltpu.VMEM((4, 4) + block, BF16),
             pltpu.VMEM((2, 4) + block, BF16),
             dma((2,)), dma((2,)), dma((2,)), dma((2,)), dma((2,)), dma((4,)), dma((4,)),
-            dma((4, 4)), dma((4, 4)), dma((3, 4)), dma((3, 4)),
+            dma((4, 4)), dma((4, 4)), dma((3, 4, 2)), dma((3, 4, 2)),
             dma((3, 4, 3)), dma((3, 4, 2)), dma((3, 4, 2)),
             dma((4, 4, 3)), dma((4, 4)), dma((2, 4)),
         ],

time: 329 us -> 319 us (0.970)
  Pallas kernels: 325 us -> 315 us
    pallas_call x1, Pallas kernels: 325 us -> 315 us  [chain(): pl.pallas_call(chain_kernel, out_shape=jax.ShapeDtypeStruct(tile.shape, B...]
where the time goes in v2:
time: 319 us; the launch traced here: 317 us
  Pallas kernels  315 us (99%)
    pallas_call x1, Pallas kernels, chain(): pl.pallas_call(chain_kernel, out_shape=jax.ShapeDtypeStruct(tile.shape, B...  315 us

profile of v2, /device:TPU:18, one launch (start us, length us, event | category | flops | bytes accessed | tf_op | source)
XLA Modules:
  0.0 317.5 jit_solution(14722121222627886697)
XLA Ops:
  0.0 315.2 %shard_map.37 = bf16[2048,256]{1,0:T(8,128)(2,1)} custom-call(bf16[2048,1024]{1,0:T(8,128)(2,1)} %bitcast.5, bf16[2048,1024]{1,0:T(8,128)(2,1)} %bitcast.6, bf16[2048,256]{1,0:T(8,128)(2,1)} %bitcast.7), custom_call_target="tpu_custom_call" | custom-call | tf_op jit(solution)/shard_map/pallas_call | solution.py:446
  315.2 2.3 copy.5

commit v3 on v2

--- a/solution.py
+++ b/solution.py
@@ -103,7 +103,7 @@
 
 def chain_kernel(
     refl, trans, shots, out, ops, inbox, faces, kept, stage, parts, far, near, far_last, near_last,
-    load_sem, core_send, core_recv, cross_send, cross_recv, init_send, init_recv, face_send, face_recv,
+    load_sem, home_sem, core_send, core_recv, cross_send, cross_recv, init_send, init_recv, face_send, face_recv,
     part_send, part_recv, col_send, far_recv, near_recv,
     last_send, last_far_recv, last_near_recv,
 ):
@@ -116,6 +116,7 @@
     high = z // 2
     end = (z == 0) | (z == 3)
     inner = (z == 1) | (z == 2)
+    home = x == high
 
     def blk(k):
         return k + high * (3 - 2 * k)
@@ -143,12 +144,26 @@
         copy.start()
 
     def shot_block(b, c):
-        return shots.at[pl.ds(b * depth, depth), pl.ds(pl.multiple_of(c * lanes, lanes), lanes)]
-
-    def cross(b):
-        return remote(
-            shot_block(b, other_x), inbox.at[b], cross_send.at[b], cross_recv.at[b], row=other_x
-        )
+        return shots.at[pl.ds(pl.multiple_of(b * depth, depth), depth), pl.ds(pl.multiple_of(c * lanes, lanes), lanes)]
+
+    def outer(j, at):
+        return at if j == 0 else 1 - at
+
+    def cross(j):
+        return remote(
+            shot_block(outer(j, x), other_x), inbox.at[j], cross_send.at[j], cross_recv.at[j],
+            row=other_x,
+        )
+
+    def near_home():
+        return remote(
+            shot_block(z % 2, x), faces.at[z, x], face_send.at[0, z], face_recv.at[0, z],
+            row=other_x,
+        )
+
+    home_load = pltpu.make_async_copy(
+        shot_block(z % 2, other_x), faces.at[z, other_x], home_sem.at[0]
+    )
 
     def hand_on(source, b, at, to, act):
         @pl.when(to == z)
@@ -161,16 +176,23 @@
             copy = remote(source, faces.at[z, x], init_send.at[at], init_recv.at[z], col=to)
             copy.start() if act == "start" else copy.wait_send()
 
-    def own_block(b, act):
-        hand_on(shot_block(b, x), b, b, 2 * x + b, act)
-
-    def crossed_block(b, act):
-        hand_on(inbox.at[b], b, 2 + b, 2 * other_x + b, act)
-
-    for b in range(2):
-        cross(b).start()
-    for b in range(2):
-        own_block(b, "start")
+    def own_block(j, act):
+        b = outer(j, x)
+        hand_on(shot_block(b, x), b, j, 2 * x + b, act)
+
+    def crossed_block(j, act):
+        hand_on(inbox.at[j], j, 2 + j, 2 * other_x + outer(j, other_x), act)
+
+    cross(0).start()
+
+    @pl.when(home)
+    def _():
+        near_home().start()
+        home_load.start()
+
+    cross(1).start()
+    for j in range(2):
+        own_block(j, "start")
 
     swaps = [
         remote(refl, ops.at[1], core_send.at[0], core_recv.at[0], slab=other_slab),
@@ -205,21 +227,32 @@
 
     def gather(g):
         pltpu.make_async_copy(faces.at[g, x], faces.at[g, x], init_recv.at[g]).wait()
-        face_copy(0, g).start()
+
+        @pl.when(z != g)
+        def _():
+            face_copy(0, g).start()
 
     tile = min(depth, 512)
     per = depth // tile
 
-    def multiply(p, g):
-        if p == 0 and g == ORDER[0]:
-            loads[0].wait()
-        if p == 1 and g == ORDER[0]:
-            swaps[0].wait_recv()
-        if p == 2 and g == ORDER[0]:
-            loads[1].wait()
-        if p == LAST and g == ORDER[0]:
-            swaps[1].wait_recv()
-        face_wait(p, g)
+    def multiply(p, g, opening):
+        if opening:
+            if p % 2:
+                swaps[p // 2].wait_recv()
+            else:
+                loads[p // 2].wait()
+        if p == 0:
+            mine = home & (z == g)
+
+            @pl.when(mine)
+            def _():
+                home_load.wait()
+
+            @pl.when(jnp.logical_not(mine))
+            def _():
+                face_wait(0, g)
+        else:
+            face_wait(p, g)
         if p < LAST:
             if p > 0:
                 for j in range(2):
@@ -339,7 +372,7 @@
                     parts[1, g, b] = (
                         parts[1, g, b].astype(F32) + far_last[g, b].astype(F32)
                     ).astype(BF16)
-                    last_near(g, b, 1, jnp.int32(g)).start()
+                    last_near(g, b, 1, g).start()
 
             return
 
@@ -364,7 +397,12 @@
             + near[p % 2, g, 0].astype(F32)
             + near[p % 2, g, 1].astype(F32)
         )
-        face_copy(p, g).wait_send()
+        if p == 0:
+            @pl.when(home | (z != g))
+            def _():
+                face_copy(p, g).wait_send()
+        else:
+            face_copy(p, g).wait_send()
         if p == 0:
             kept[g] = total.astype(BF16)
         if p == 2:
@@ -372,22 +410,30 @@
         faces[g, x] = total.astype(BF16)
         face_copy(p + 1, g).start()
 
-    order = [(p, g) for p in range(LAST + 1) for g in ORDER]
-    for g in ORDER[:2]:
-        gather(g)
-    multiply(*order[0])
-    for g in ORDER[2:]:
-        gather(g)
+    order = [(0, blk(g)) for g in ORDER]
+    order += [(p, g) for p in range(1, LAST) for g in ORDER]
+    order += [(LAST, blk(g)) for g in (0, 3, 2, 1)]
     count = len(order)
+
+    def advance(t):
+        multiply(*order[t], opening=t % 4 == 0)
+
+    gather(order[0][1])
+    advance(0)
+    for t in range(1, 4):
+        gather(order[t][1])
     for t in range(count + 2):
+        if 0 <= t - 1 < count:
+            merge(*order[t - 1])
+        if t in (2, 4):
+            for g in ORDER[t - 2 : t]:
+                finish(0, g)
+        if 4 <= t - 2 < count:
+            finish(*order[t - 2])
         if t < count:
             begin(*order[t])
-        if 0 <= t - 1 < count:
-            merge(*order[t - 1])
         if t + 1 < count:
-            multiply(*order[t + 1])
-        if 0 <= t - 2 < count:
-            finish(*order[t - 2])
+            advance(t + 1)
 
     for g in range(4):
         @pl.when(z == g)
@@ -459,7 +505,7 @@
             pltpu.VMEM((2, 4, 2) + block, BF16),
             pltpu.VMEM((4, 4) + block, BF16),
             pltpu.VMEM((2, 4) + block, BF16),
-            dma((2,)), dma((2,)), dma((2,)), dma((2,)), dma((2,)), dma((4,)), dma((4,)),
+            dma((2,)), dma((1,)), dma((2,)), dma((2,)), dma((2,)), dma((2,)), dma((4,)), dma((4,)),
             dma((4, 4)), dma((4, 4)), dma((3, 4, 2)), dma((3, 4, 2)),
             dma((3, 4, 3)), dma((3, 4, 2)), dma((3, 4, 2)),
             dma((4, 4, 3)), dma((4, 4)), dma((2, 4)),

time: 319 us -> 314 us (0.984)
    pallas_call x1, Pallas kernels: 315 us -> 312 us  [chain(): pl.pallas_call(chain_kernel, out_shape=jax.ShapeDtypeStruct(tile.shape, B...]
where the time goes in v3:
time: 314 us
  Pallas kernels  312 us (99%)
    pallas_call x1, Pallas kernels, chain(): pl.pallas_call(chain_kernel, out_shape=jax.ShapeDtypeStruct(tile.shape, B...  312 us

profile of v3, /device:TPU:18, one launch (start us, length us, event | category | flops | bytes accessed | tf_op | source)
XLA Modules:
  0.0 314.1 jit_solution(12044786508633185689)
XLA Ops:
  0.0 311.9 %shard_map.37 = bf16[2048,256]{1,0:T(8,128)(2,1)} custom-call(bf16[2048,1024]{1,0:T(8,128)(2,1)} %bitcast.5, bf16[2048,1024]{1,0:T(8,128)(2,1)} %bitcast.6, bf16[2048,256]{1,0:T(8,128)(2,1)} %bitcast.7), custom_call_target="tpu_custom_call" | custom-call | tf_op jit(solution)/shard_map/pallas_call | solution.py:492
  311.9 2.3 copy.5

commit v4 on v3

--- a/solution.py
+++ b/solution.py
@@ -277,10 +277,28 @@
             return block
 
         for j in range(2):
-            lax.fori_loop(0, per, body, turn(j))
+            lax.fori_loop(0, per, body, turn(j) if p < LAST else j)
             if p < LAST:
                 part_copy(p, g, j, x).start()
                 send_block(p, g, 2 * x + turn(j))
+            else:
+                send_last(g, (j, 2 + j))
+
+    def send_last(g, blocks):
+        @pl.when(end & is_blk(g, 2, 3))
+        def _():
+            for b in blocks:
+                last_far(g, b, blk(1)).start()
+
+        @pl.when(end & is_blk(g, 1))
+        def _():
+            for b in blocks:
+                last_near(g, b, 0, blk(1)).start()
+
+        @pl.when(inner & is_blk(g, 0))
+        def _():
+            for b in blocks:
+                last_near(g, b, 0, blk(0)).start()
 
     def send_block(p, g, block):
         for copy, k in zip(end_copies(p, g), (3, 2, 1)):
@@ -343,21 +361,6 @@
 
     def begin(p, g):
         if p == LAST:
-            @pl.when(end & is_blk(g, 2, 3))
-            def _():
-                for b in range(4):
-                    last_far(g, b, blk(1)).start()
-
-            @pl.when(end & is_blk(g, 1))
-            def _():
-                for b in range(4):
-                    last_near(g, b, 0, blk(1)).start()
-
-            @pl.when(inner & is_blk(g, 0))
-            def _():
-                for b in range(4):
-                    last_near(g, b, 0, blk(0)).start()
-
             return
         for j in range(2):
             part_copy(p, g, j, other_x).wait_recv()
@@ -367,7 +370,7 @@
         if p == LAST:
             @pl.when(inner & is_blk(g, 2, 3))
             def _():
-                for b in range(4):
+                for b in (0, 2, 1, 3):
                     last_far(g, b, blk(1)).wait_recv()
                     parts[1, g, b] = (
                         parts[1, g, b].astype(F32) + far_last[g, b].astype(F32)
@@ -412,7 +415,7 @@
 
     order = [(0, blk(g)) for g in ORDER]
     order += [(p, g) for p in range(1, LAST) for g in ORDER]
-    order += [(LAST, blk(g)) for g in (0, 3, 2, 1)]
+    order += [(LAST, blk(g)) for g in (3, 0, 2, 1)]
     count = len(order)
 
     def advance(t):
@@ -423,13 +426,13 @@
     for t in range(1, 4):
         gather(order[t][1])
     for t in range(count + 2):
-        if 0 <= t - 1 < count:
-            merge(*order[t - 1])
-        if t in (2, 4):
-            for g in ORDER[t - 2 : t]:
+        if t in (3, 5):
+            for g in ORDER[t - 3 : t - 1]:
                 finish(0, g)
         if 4 <= t - 2 < count:
             finish(*order[t - 2])
+        if 0 <= t - 1 < count:
+            merge(*order[t - 1])
         if t < count:
             begin(*order[t])
         if t + 1 < count:
@@ -438,7 +441,7 @@
     for g in range(4):
         @pl.when(z == g)
         def _():
-            for b in range(4):
+            for b in (0, 2, 1, 3):
                 for at in range(2):
                     last_near(g, b, at, z).wait_recv()
                 c, h = b // 2, b % 2

time: 314 us -> 313 us (level)
  Pallas kernels: 312 us -> 308 us
    pallas_call x1, Pallas kernels: 312 us -> 308 us  [chain(): pl.pallas_call(chain_kernel, out_shape=jax.ShapeDtypeStruct(tile.shape, B...]
where the time goes in v4:
time: 313 us; the launch traced here: 311 us
  Pallas kernels  308 us (98%)
    pallas_call x1, Pallas kernels, chain(): pl.pallas_call(chain_kernel, out_shape=jax.ShapeDtypeStruct(tile.shape, B...  308 us

profile of v4, /device:TPU:18, one launch (start us, length us, event | category | flops | bytes accessed | tf_op | source)
XLA Modules:
  0.0 310.6 jit_solution(11118205137406789266)
XLA Ops:
  0.0 308.3 %shard_map.37 = bf16[2048,256]{1,0:T(8,128)(2,1)} custom-call(bf16[2048,1024]{1,0:T(8,128)(2,1)} %bitcast.5, bf16[2048,1024]{1,0:T(8,128)(2,1)} %bitcast.6, bf16[2048,256]{1,0:T(8,128)(2,1)} %bitcast.7), custom_call_target="tpu_custom_call" | custom-call | tf_op jit(solution)/shard_map/pallas_call | solution.py:495
  308.3 2.3 copy.5

commit v5 on v4

--- a/solution.py
+++ b/solution.py
@@ -102,10 +102,10 @@
 
 
 def chain_kernel(
-    refl, trans, shots, out, ops, inbox, faces, kept, stage, parts, far, near, far_last, near_last,
+    refl, trans, shots, out, total_out, ops, inbox, faces, kept, stage, parts, far, near, far_last, near_last,
     load_sem, home_sem, core_send, core_recv, cross_send, cross_recv, init_send, init_recv, face_send, face_recv,
     part_send, part_recv, col_send, far_recv, near_recv,
-    last_send, last_far_recv, last_near_recv,
+    last_send, last_far_recv, last_near_recv, out_sem,
 ):
     s, x, z = lax.axis_index("slab"), lax.axis_index("row"), lax.axis_index("col")
     other_slab = s + 1 - 2 * (s % 2)
@@ -438,6 +438,9 @@
         if t + 1 < count:
             advance(t + 1)
 
+    def out_part(ref, h, c):
+        return ref.at[pl.ds(h * depth, depth), pl.ds(c * lanes, lanes)]
+
     for g in range(4):
         @pl.when(z == g)
         def _():
@@ -445,11 +448,12 @@
                 for at in range(2):
                     last_near(g, b, at, z).wait_recv()
                 c, h = b // 2, b % 2
-                out[pl.ds(h * depth, depth), pl.ds(c * lanes, lanes)] = (
+                total_out[pl.ds(h * depth, depth), pl.ds(c * lanes, lanes)] = (
                     parts[1, g, b].astype(F32)
                     + near_last[0, b].astype(F32)
                     + near_last[1, b].astype(F32)
                 ).astype(BF16)
+                pltpu.make_async_copy(out_part(total_out, h, c), out_part(out, h, c), out_sem.at[b]).start()
 
     for g in range(4):
         settle(LAST - 1, g)
@@ -483,6 +487,9 @@
         cross(b).wait_send()
         own_block(b, "wait")
         crossed_block(b, "wait")
+    for b in range(4):
+        c, h = b // 2, b % 2
+        pltpu.make_async_copy(out_part(total_out, h, c), out_part(out, h, c), out_sem.at[b]).wait()
 
 
 def chain(reflection, transmission, shots):
@@ -496,8 +503,9 @@
         chain_kernel,
         out_shape=jax.ShapeDtypeStruct(tile.shape, BF16),
         in_specs=[hbm] * 3,
-        out_specs=pl.BlockSpec(memory_space=pltpu.VMEM),
+        out_specs=hbm,
         scratch_shapes=[
+            pltpu.VMEM(tile.shape, BF16),
             pltpu.VMEM((4, height, inner), BF16),
             pltpu.VMEM((2,) + block, BF16),
             pltpu.VMEM((4, 2) + block, BF16),
@@ -511,7 +519,7 @@
             dma((2,)), dma((1,)), dma((2,)), dma((2,)), dma((2,)), dma((2,)), dma((4,)), dma((4,)),
             dma((4, 4)), dma((4, 4)), dma((3, 4, 2)), dma((3, 4, 2)),
             dma((3, 4, 3)), dma((3, 4, 2)), dma((3, 4, 2)),
-            dma((4, 4, 3)), dma((4, 4)), dma((2, 4)),
+            dma((4, 4, 3)), dma((4, 4)), dma((2, 4)), dma((4,)),
         ],
         compiler_params=pltpu.CompilerParams(
             collective_id=0, has_side_effects=True, vmem_limit_bytes=60 << 20

time: 313 us -> 313 us (level)
  no operation moved by 1% of the time
where the time goes in v5:
time: 313 us; the launch traced here: 310 us
  Pallas kernels  308 us (98%)
    pallas_call x1, Pallas kernels, chain(): pl.pallas_call(chain_kernel, out_shape=jax.ShapeDtypeStruct(tile.shape, B...  308 us

profile of v5, /device:TPU:18, one launch (start us, length us, event | category | flops | bytes accessed | tf_op | source)
XLA Modules:
  0.0 310.2 jit_solution(7594328095104694816)
XLA Ops:
  0.0 307.9 %shard_map.37 = bf16[2048,256]{1,0:T(8,128)(2,1)} custom-call(bf16[2048,1024]{1,0:T(8,128)(2,1)} %bitcast.5, bf16[2048,1024]{1,0:T(8,128)(2,1)} %bitcast.6, bf16[2048,256]{1,0:T(8,128)(2,1)} %bitcast.7), custom_call_target="tpu_custom_call" | custom-call | tf_op jit(solution)/shard_map/pallas_call | solution.py:502
  307.9 2.3 copy.5

commit v6 on v5

--- a/solution.py
+++ b/solution.py
@@ -96,7 +96,7 @@
 
 
 F32, BF16 = jnp.float32, jnp.bfloat16
-ORDER = (0, 3, 1, 2)
+ORDER = (0, 3, 2, 1)
 LAST = 3
 MESH = pl.DeviceIdType.MESH
 
@@ -383,7 +383,7 @@
         def _():
             arrive = end_copies(p, g)
             leave = inner_copies(p, g)
-            for at, k in ((0, 3), (1, 2)):
+            for at, k in ((1, 2), (0, 3)):
                 arrive[at].wait_recv()
                 parts[p % 2, g, blk(k)] = (
                     parts[p % 2, g, blk(k)].astype(F32) + far[p % 2, g, at].astype(F32)
@@ -522,7 +522,7 @@
             dma((4, 4, 3)), dma((4, 4)), dma((2, 4)), dma((4,)),
         ],
         compiler_params=pltpu.CompilerParams(
-            collective_id=0, has_side_effects=True, vmem_limit_bytes=60 << 20
+            collective_id=0, has_side_effects=True, vmem_limit_bytes=48 << 20
         ),
     )(refl, trans, tile)
     return out[None]

time: 313 us -> 312 us (level)
  no operation moved by 1% of the time
where the time goes in v6:
time: 312 us; the launch traced here: 310 us
  Pallas kernels  307 us (98%)
    pallas_call x1, Pallas kernels, chain(): pl.pallas_call(chain_kernel, out_shape=jax.ShapeDtypeStruct(tile.shape, B...  307 us

profile of v6, /device:TPU:18, one launch (start us, length us, event | category | flops | bytes accessed | tf_op | source)
XLA Modules:
  0.0 309.5 jit_solution(2161504701965120535)
XLA Ops:
  0.0 0.0 copy-start
  0.0 1.2 copy-done
  1.2 307.3 %shard_map.37 = bf16[2048,256]{1,0:T(8,128)(2,1)S(1)} custom-call(bf16[2048,1024]{1,0:T(8,128)(2,1)} %bitcast.6, bf16[2048,1024]{1,0:T(8,128)(2,1)} %bitcast.7, bf16[2048,256]{1,0:T(8,128)(2,1)S(1)} %bitcast.5), custom_call_target="tpu_custom_call" | custom-call | tf_op jit(solution)/shard_map/pallas_call | solution.py:502
  308.5 1.0 copy.5
Async XLA Ops:
  0.0 1.2 copy-start
